TPU v7x, 32 devices: a whole 2x2x4 slice. The times are simulated.
32 devices in a mesh: grp: 2 (over y), trade: 4 (over z), date: 2 (over x), path: 2 (over core).
Axes of the slice: x: 2, y: 2, z: 4, core: 2. Of those that a mesh axis runs over, the one named last changes fastest.
Arguments:
- driver_increments: float32 [16, 256, 128], P(('grp', 'date'), 'path'), parts along dimension 0, may hold values from -4 to 4
- persistence_ratio: float32 [16, 128], P(('grp', 'date')), parts along dimension 0, may hold values from 0 to 1, as said below
- deal_sensitivity: bfloat16 [128, 65536], P(None, ('grp', 'trade')), parts along dimension 1, may hold values from -0.5 to 0.5
- signed_notional: float32 [65536], P(('grp', 'trade')), parts along dimension 0, may hold values from -0.4 to 0.4
- batch_obligor: int32 [512], P(('grp', 'trade')), parts along dimension 0, may hold values from 0 to 127, as said below
- collateral_ceiling: float32 [256], P(('grp', 'trade')), parts along dimension 0, may hold values from -1 to 1
- default_discount_mass: float32 [16, 128], P(('grp', 'date'), 'trade'), parts along dimension 0, may hold values from 0.1 to 1
Outputs:
- exposure_profile: float32 [16, 128], P(('grp', 'date'), 'trade'), parts along dimension 0
- shock_gradient: float32 [16, 256, 128], P(('grp', 'date'), 'path'), parts along dimension 0
There are 2 independent parts, one for each index of `grp`. A program takes and returns all parts, laid end to end along the dimension named above; each array names one. Nothing has to cross between parts.
Inputs may be any that keep to these rules, and one draw needn't show every extreme that they name: `persistence_ratio`: strictly between 0 and 1. `batch_obligor`: counterparty c belongs to trade shard c // 32. Of the 64 trade blocks of one trade shard, at most 32 have counterparties on any one trade shard, and in every trade shard some counterparty shard receives exactly 32 of them.
All inputs are finite; a program needn't handle non-finite values.
Results may differ from a plain program's by a relative error of at most 0.0019.
Values sent between devices are 32-bit elements; how exact they have to be, the bound alone decides.
No kernel may reach another device: no remote copies, remote signals or barrier semaphores. Data moves between devices by JAX's collectives and lax.ppermute only.
A program may use at most 64 MiB of HBM per device.

v0:
```python
import jax
import jax.numpy as jnp
from jax import lax
from jax.sharding import PartitionSpec as P

block_width = 128
cluster_extent = 512
highest = lax.Precision.HIGHEST


def entering(value, axis, combine, identity, reverse):
    length, index = (lax.axis_size(axis), lax.axis_index(axis))
    everything = jax.tree.map(lambda part: lax.all_gather(part, axis), value)
    start = jax.tree.map(
        lambda part, zero: jnp.broadcast_to(jnp.asarray(zero, part.dtype), part.shape),
        value,
        identity,
    )

    def hop(k, before):
        at = length - 1 - k if reverse else k
        reached = at > index if reverse else at < index
        new = combine(before, jax.tree.map(lambda part: part[at], everything))
        return jax.tree.map(lambda a, b: jnp.where(reached, a, b), new, before)

    return lax.fori_loop(0, length, hop, start)


def compose(earlier, later):
    return (later[0] * earlier[0], later[0] * earlier[1] + later[1])


def reverse_chain(direct, persistence_ratio):
    date_count = direct.shape[0]
    factor_gain = jnp.ones((direct.shape[2],), jnp.float32)
    message = jnp.zeros(direct.shape[1:], jnp.float32)
    for date_step in reversed(range(date_count)):
        message = persistence_ratio[date_step][None, :] * (direct[date_step] + message)
        factor_gain = persistence_ratio[date_step] * factor_gain
    identity = (jnp.ones_like(factor_gain), jnp.zeros_like(message))
    _, arriving = entering((factor_gain, message), "date", compose, identity, True)
    adjoints = []
    message = arriving
    for date_step in reversed(range(date_count)):
        adjoint = direct[date_step] + message
        adjoints.append(adjoint)
        message = persistence_ratio[date_step][None, :] * adjoint
    return jnp.stack(adjoints[::-1])


def shards(
    driver_increments,
    persistence_ratio,
    deal_sensitivity,
    signed_notional,
    batch_obligor,
    collateral_ceiling,
    default_discount_mass,
):
    date_count, path_count, factor_count = driver_increments.shape
    factor_gain = jnp.ones((factor_count,), jnp.float32)
    carried = jnp.zeros((path_count, factor_count), jnp.float32)
    for date_step in range(date_count):
        carried = persistence_ratio[date_step][None, :] * carried + driver_increments[date_step]
        factor_gain = persistence_ratio[date_step] * factor_gain
    identity = (jnp.ones_like(factor_gain), jnp.zeros_like(carried))
    _, arriving = entering((factor_gain, carried), "date", compose, identity, False)
    states = []
    carried = arriving
    for date_step in range(date_count):
        carried = persistence_ratio[date_step][None, :] * carried + driver_increments[date_step]
        states.append(carried)
    row_count = date_count * path_count
    state_bf = jnp.stack(states).reshape(row_count, factor_count).astype(jnp.bfloat16)
    deal_ordinal = deal_sensitivity.shape[1]
    block_count = deal_ordinal // block_width
    cluster_ordinal = deal_ordinal // cluster_extent
    per_group = cluster_extent // block_width

    def value_group(group_index, block_sums):
        opening_offset = group_index * cluster_extent
        sensitivity_portion = lax.dynamic_slice_in_dim(
            deal_sensitivity, opening_offset, cluster_extent, 1
        )
        size_part = lax.dynamic_slice_in_dim(signed_notional, opening_offset, cluster_extent, 0)
        linear = jnp.dot(state_bf, sensitivity_portion, preferred_element_type=jnp.float32)
        trade_value = jax.nn.softplus(linear) * size_part[None, :]
        summed = trade_value.reshape(row_count, per_group, block_width).sum(axis=2)
        return lax.dynamic_update_slice_in_dim(block_sums, summed.T, group_index * per_group, 0)

    block_sums = lax.fori_loop(
        0, cluster_ordinal, value_group, jnp.zeros((block_count, row_count), jnp.float32)
    )
    cpty_dev = collateral_ceiling.shape[0]
    shard_count = lax.axis_size("trade")
    ownership = (
        batch_obligor[:, None] == jnp.arange(cpty_dev * shard_count, dtype=jnp.int32)[None, :]
    ).astype(jnp.float32)
    partial_value = lax.dot_general(
        ownership, block_sums, (((0,), (0,)), ((), ())), precision=highest
    )
    netted = lax.psum_scatter(partial_value, "trade", scatter_dimension=0, tiled=True)
    shifted = netted - collateral_ceiling[:, None]
    exposure = jax.nn.softplus(shifted).reshape(cpty_dev, date_count, path_count)
    path_total = lax.psum(jnp.sum(exposure, axis=2).T, "path")
    exposure_profile = path_total / (path_count * lax.axis_size("path"))
    net_adjoint = (
        default_discount_mass.T[:, :, None]
        * jax.nn.sigmoid(shifted).reshape(cpty_dev, date_count, path_count)
    ).reshape(cpty_dev, row_count)
    gathered = lax.all_gather(net_adjoint, "trade", axis=0, tiled=True)
    block_adjoint = jnp.dot(ownership, gathered, precision=highest)

    def pull_group(group_index, running):
        opening_offset = group_index * cluster_extent
        sensitivity_portion = lax.dynamic_slice_in_dim(
            deal_sensitivity, opening_offset, cluster_extent, 1
        )
        size_part = lax.dynamic_slice_in_dim(signed_notional, opening_offset, cluster_extent, 0)
        linear = jnp.dot(state_bf, sensitivity_portion, preferred_element_type=jnp.float32)
        slope_term = jax.nn.sigmoid(linear) * size_part[None, :]
        upstream = lax.dynamic_slice_in_dim(block_adjoint, group_index * per_group, per_group, 0)
        value_adjoint = (
            (upstream.T[:, :, None] * slope_term.reshape(row_count, per_group, block_width))
            .reshape(row_count, cluster_extent)
            .astype(jnp.bfloat16)
        )
        product = lax.dot_general(
            value_adjoint,
            sensitivity_portion,
            (((1,), (1,)), ((), ())),
            preferred_element_type=jnp.float32,
        )
        return running + product

    direct = lax.fori_loop(
        0, cluster_ordinal, pull_group, jnp.zeros((row_count, factor_count), jnp.float32)
    )
    direct = direct.reshape(date_count, path_count, factor_count)
    summed = lax.psum(direct, "trade")
    shock_gradient = reverse_chain(summed, persistence_ratio)
    return (exposure_profile, shock_gradient)


def solution(mesh):
    return jax.shard_map(
        shards,
        mesh=mesh,
        in_specs=(
            P(("grp", "date"), "path", None),
            P(("grp", "date"), None),
            P(None, ("grp", "trade")),
            P(("grp", "trade")),
            P(("grp", "trade")),
            P(("grp", "trade")),
            P(("grp", "date"), "trade"),
        ),
        out_specs=(P(("grp", "date"), "trade"), P(("grp", "date"), "path", None)),
        check_vma=False,
    )
```

profile of v0, /device:TPU:0, one launch (start us, length us, event | category | flops | bytes accessed | tf_op | source)
XLA Modules:
  0.0 200.2 jit_solution(7079904627721618631)
XLA Ops:
  8.8 5.1 %all-gather = f32[2,1,128]{2,1,0:T(1,128)S(1)} all-gather(f32[1,1,128]{2,1,0:T(1,128)S(1)} %get-tuple-element.550), channel_id=1, replica_groups=mesh['grp'=2,'trade'=4,'date'=2,'path'=2] {'date'}, dimensions={0}, use_global_device_ids=true | all-gather | bytes 1536 | tf_op jit(solution)/shard_map/all_gather | solution.py:13
  14.8 4.9 %all_gather.20 = f32[2,128,128]{2,1,0:T(8,128)S(1)} all-gather(f32[1,128,128]{2,1,0:T(8,128)S(1)} %multiply_add_fusion), channel_id=1, replica_groups=mesh['grp'=2,'trade'=4,'date'=2,'path'=2] {'date'}, dimensions={0}, use_global_device_ids=true | all-gather | bytes 196608 | tf_op jit(solution)/shard_map/all_gather | solution.py:13
  20.9 41.0 %while.57 = (s32[]{:T(128)}, f32[64,512]{1,0:T(8,128)S(1)}, bf16[128,8192]{1,0:T(8,128)(2,1)}, bf16[512,128]{1,0:T(8,128)(2,1)S(1)}, f32[8192]{0:T(1024)}, /*ind...) while((s32[]{:T(128)}, f32[64,512]{1,0:T(8,128)S(1)}, ...), condition=%wide.region_4.5_spmd, body=%wide.region_2.4_spmd.sunk | while | flops 69203976 | bytes 293085 | solution.py:91
  21.7 1.8 bitcast_reduce_fusion.2
  24.2 1.8 bitcast_reduce_fusion.2
  26.8 1.8 bitcast_reduce_fusion.2
  29.4 1.8 bitcast_reduce_fusion.2
  31.9 1.8 bitcast_reduce_fusion.2
  34.5 1.8 bitcast_reduce_fusion.2
  37.0 1.8 bitcast_reduce_fusion.2
  39.6 1.7 bitcast_reduce_fusion.2
  42.2 1.8 bitcast_reduce_fusion.2
  44.7 1.8 bitcast_reduce_fusion.2
  47.3 1.8 bitcast_reduce_fusion.2
  49.8 1.7 bitcast_reduce_fusion.2
  52.4 1.8 bitcast_reduce_fusion.2
  55.0 1.8 bitcast_reduce_fusion.2
  57.5 1.8 bitcast_reduce_fusion.2
  60.1 1.8 bitcast_reduce_fusion.2
  63.1 21.4 %reduce-scatter.2.cloned.1.call-done = f32[32,512]{1,0:T(8,128)} async-done(((f32[128,512]{1,0:T(8,128)}), f32[32,512]{1,0:T(8,128)}) %reduce-scatter.2.cloned.1.call-update) | async-done | bytes 65552 | tf_op jit(solution)/shard_map/reduce_scatter | solution.py:102
  85.6 13.8 %all_gather.21 = f32[128,512]{1,0:T(8,128)S(1)} all-gather(f32[32,512]{1,0:T(8,128)S(1)} %get-tuple-element.544), channel_id=1, replica_groups=mesh['grp'=2,'trade'=4,'date'=2,'path'=2] {'trade'}, dimensions={0}, use_global_device_ids=true | all-gather | bytes 327680 | tf_op jit(solution)/shard_map/all_gather | solution.py:111
  99.7 50.3 %while.59 = (s32[]{:T(128)}, f32[512,128]{1,0:T(8,128)S(1)}, f32[64,512]{1,0:T(8,128)S(1)}, bf16[128,8192]{1,0:T(8,128)(2,1)}, bf16[512,128]{1,0:T(8,128)(2,1)S(...) while((s32[]{:T(128)}, f32[512,128]{1,0:T(8,128)S(1)}, ...), condition=%wide.region_9.10_spmd.clone, body=%wide.region_8.9_spmd.clone.sunk | while | flops 135921680 | bytes 3063530 | solution.py:136
  101.3 1.6 fusion.50
  104.4 1.6 fusion.50
  113.8 1.6 fusion.50
  129.5 1.6 fusion.50
  132.7 1.6 fusion.50
  145.3 1.6 fusion.50
  150.8 4.2 %all-gather.1 = f32[2,1,128]{2,1,0:T(1,128)S(1)} all-gather(f32[1,1,128]{2,1,0:T(1,128)S(1)} %get-tuple-element.546), channel_id=1, replica_groups=mesh['grp'=2,'trade'=4,'date'=2,'path'=2] {'date'}, dimensions={0}, use_global_device_ids=true | all-gather | bytes 1536 | tf_op jit(solution)/shard_map/all_gather | solution.py:13
  155.1 3.4 %psum.14 = f32[4,32]{0,1:T(8,128)S(1)} all-reduce(f32[4,32]{0,1:T(8,128)S(1)} %bitcast.153), channel_id=1, replica_groups=mesh['grp'=2,'trade'=4,'date'=2,'path'=2] {'path'}, use_global_device_ids=true, to_apply=%region_7.8 | all-reduce | flops 128 | bytes 1024 | tf_op jit(solution)/shard_map/psum | solution.py:105
  159.1 25.7 %all-reduce.2.cloned.1.call-done = f32[4,128,128]{2,1,0:T(8,128)} async-done(((f32[4,128,128]{2,1,0:T(8,128)}), f32[4,128,128]{2,1,0:T(8,128)}) %all-reduce.2.cloned.1.call-update) | async-done | bytes 262160 | tf_op jit(solution)/shard_map/psum | solution.py:140
  185.8 4.9 %all_gather.23 = f32[2,128,128]{2,1,0:T(8,128)S(1)} all-gather(f32[1,128,128]{2,1,0:T(8,128)S(1)} %add_multiply_fusion), channel_id=1, replica_groups=mesh['grp'=2,'trade'=4,'date'=2,'path'=2] {'date'}, dimensions={0}, use_global_device_ids=true | all-gather | bytes 196608 | tf_op jit(solution)/shard_map/all_gather | solution.py:13
  (153 shorter events, 63.8 us)
Async XLA Ops:
  7.2 13.6 %copy-start = (f32[4,128,128]{2,1,0:T(8,128)S(1)}, f32[4,128,128]{2,1,0:T(8,128)}, u32[]{:S(2)}) copy-start(f32[4,128,128]{2,1,0:T(8,128)} %param.15) | copy-start | bytes 786436
  7.2 77.3 %reduce-scatter.2.cloned.1.call-start = ((), (), s32[]{:S(2)}) async-start(), calls=%async_computation.1 | async-start | bytes 327680 | tf_op jit(solution)/shard_map/reduce_scatter | solution.py:102
  20.8 41.0 %copy-start.2 = (s32[64]{0:T(128)S(1)}, s32[64]{0:T(128)}, u32[]{:S(2)}) copy-start(s32[64]{0:T(128)} %param.19) | copy-start | bytes 772
  20.9 42.2 %copy-start.3 = (f32[4,32]{1,0:T(4,128)S(1)}, f32[4,32]{1,0:T(4,128)}, u32[]{:S(2)}) copy-start(f32[4,32]{1,0:T(4,128)} %param.21) | copy-start | bytes 1540
  20.9 63.7 %copy-start.4 = (f32[32]{0:T(128)S(1)}, f32[32]{0:T(128)}, u32[]{:S(2)}) copy-start(f32[32]{0:T(128)} %param.20) | copy-start | bytes 388
  63.0 121.9 %all-reduce.2.cloned.1.call-start = ((), (), s32[]{:S(2)}) async-start(), calls=%async_computation.2 | async-start | bytes 524288 | tf_op jit(solution)/shard_map/psum | solution.py:140
  150.0 0.7 copy-start.1
Sparse Core Ops, SparseCore 0:
  63.1 21.3 reduce-scatter.1
  150.9 33.9 all-reduce.1
where the time goes:
time: 202 us; the launch traced here: 200 us
  matrix products  54.4 us (27%)
  waiting for transfers between devices  47.1 us (23%)
  local copies, waits for them, and re-layouts  38.5 us (19%)
  blocking collectives  36.4 us (18%)
  between operations  14.2 us (7%)
  other arithmetic  8.08 us (4%)
    dot_general x16, matrix products, value_group(): jnp.dot(state_bf, sensitivity_portion, preferred_element_type=jnp.float32)  28 us
    psum x1, waiting for transfers between devices, shards(): summed = lax.psum(direct, 'trade')  25.7 us
    dot_general x16, matrix products, pull_group(): lax.dot_general(value_adjoint, sensitivity_portion, (((1,), (1,)), ((), (...  25.1 us
    reduce_scatter x1, waiting for transfers between devices, shards(): lax.psum_scatter(partial_value, 'trade', scatter_dimension=0, tiled=True)  21.4 us
    all_gather x4, blocking collectives, entering(): everything = jax.tree.map(lambda part: lax.all_gather(part, axis), value)  19.2 us
    all_gather x1, blocking collectives, shards(): gathered = lax.all_gather(net_adjoint, 'trade', axis=0, tiled=True)  13.8 us
    dynamic_slice x16, local copies, waits for them, and re-layouts, value_group(): lax.dynamic_slice_in_dim(signed_notional, opening_offset, cluster_extent, 0)  12.2 us
    dynamic_slice x16, local copies, waits for them, and re-layouts, pull_group(): lax.dynamic_slice_in_dim(signed_notional, opening_offset, cluster_extent, 0)  12.2 us
  transfers between devices with their start and end apart: 2, of which 2 were waited for; matrix products, arithmetic and copies ran while one was open for 0% of the time, Pallas kernels for 0%

commit v1 on v0

--- a/solution.py
+++ b/solution.py
@@ -108,7 +108,15 @@
         default_discount_mass.T[:, :, None]
         * jax.nn.sigmoid(shifted).reshape(cpty_dev, date_count, path_count)
     ).reshape(cpty_dev, row_count)
-    gathered = lax.all_gather(net_adjoint, "trade", axis=0, tiled=True)
+    ways, here, hop_2 = (lax.axis_size("trade"), lax.axis_index("trade"), net_adjoint.shape[0])
+    line, have = (net_adjoint, 1)
+    while have < ways:
+        line = jnp.concatenate(
+            [line, lax.ppermute(line, "trade", [(d, (d - have) % ways) for d in range(ways)])],
+            axis=0,
+        )
+        have = 2 * have
+    gathered = jnp.roll(line, here * hop_2, axis=0)
     block_adjoint = jnp.dot(ownership, gathered, precision=highest)
 
     def pull_group(group_index, running):

time: 202 us -> 201 us (level)
  blocking collectives: 36.4 us -> 22.6 us
  waiting for transfers between devices: 47.1 us -> 58.1 us
    all_gather x1 -> x0, blocking collectives: 13.8 us -> none  [shards(): gathered = lax.all_gather(net_adjoint, 'trade', axis=0, tiled=True)]
    ppermute x0 -> x2, waiting for transfers between devices: none -> 9.79 us  [shards(): lax.ppermute(line, 'trade', [(d, (d - have) % ways) for d in range(ways)])]
  transfers between devices with their start and end apart: 2 -> 4, of which waited for: 2 -> 4; matrix products, arithmetic and copies ran while one was open for 0% -> 0% of each run, Pallas kernels for 0% -> 0%
where the time goes in v1:
time: 201 us; the launch traced here: 199 us
  waiting for transfers between devices  58.1 us (29%)
  matrix products  54.4 us (27%)
  local copies, waits for them, and re-layouts  38.5 us (19%)
  blocking collectives  22.6 us (11%)
  between operations  14.3 us (7%)
  other arithmetic  8.09 us (4%)
    dot_general x16, matrix products, value_group(): jnp.dot(state_bf, sensitivity_portion, preferred_element_type=jnp.float32)  28 us
    psum x1, waiting for transfers between devices, shards(): summed = lax.psum(direct, 'trade')  26.9 us
    dot_general x16, matrix products, pull_group(): lax.dot_general(value_adjoint, sensitivity_portion, (((1,), (1,)), ((), (...  25.1 us
    reduce_scatter x1, waiting for transfers between devices, shards(): lax.psum_scatter(partial_value, 'trade', scatter_dimension=0, tiled=True)  21.4 us
    all_gather x4, blocking collectives, entering(): everything = jax.tree.map(lambda part: lax.all_gather(part, axis), value)  19.2 us
    dynamic_slice x16, local copies, waits for them, and re-layouts, value_group(): lax.dynamic_slice_in_dim(signed_notional, opening_offset, cluster_extent, 0)  12.2 us
    dynamic_slice x16, local copies, waits for them, and re-layouts, pull_group(): lax.dynamic_slice_in_dim(signed_notional, opening_offset, cluster_extent, 0)  12.2 us
    ppermute x2, waiting for transfers between devices, shards(): lax.ppermute(line, 'trade', [(d, (d - have) % ways) for d in range(ways)])  9.79 us
  transfers between devices with their start and end apart: 4, of which 4 were waited for; matrix products, arithmetic and copies ran while one was open for 0% of the time, Pallas kernels for 0%

profile of v1, /device:TPU:0, one launch (start us, length us, event | category | flops | bytes accessed | tf_op | source)
XLA Modules:
  0.0 198.7 jit_solution(11477016559130328201)
XLA Ops:
  8.8 5.1 %all-gather = f32[2,1,128]{2,1,0:T(1,128)S(1)} all-gather(f32[1,1,128]{2,1,0:T(1,128)S(1)} %get-tuple-element.551), channel_id=1, replica_groups=mesh['grp'=2,'trade'=4,'date'=2,'path'=2] {'date'}, dimensions={0}, use_global_device_ids=true | all-gather | bytes 1536 | tf_op jit(solution)/shard_map/all_gather | solution.py:13
  14.8 4.9 %all_gather.17 = f32[2,128,128]{2,1,0:T(8,128)S(1)} all-gather(f32[1,128,128]{2,1,0:T(8,128)S(1)} %multiply_add_fusion), channel_id=1, replica_groups=mesh['grp'=2,'trade'=4,'date'=2,'path'=2] {'date'}, dimensions={0}, use_global_device_ids=true | all-gather | bytes 196608 | tf_op jit(solution)/shard_map/all_gather | solution.py:13
  20.9 41.0 %while.57 = (s32[]{:T(128)}, f32[64,512]{1,0:T(8,128)S(1)}, bf16[128,8192]{1,0:T(8,128)(2,1)}, bf16[512,128]{1,0:T(8,128)(2,1)S(1)}, f32[8192]{0:T(1024)}, /*ind...) while((s32[]{:T(128)}, f32[64,512]{1,0:T(8,128)S(1)}, ...), condition=%wide.region_4.5_spmd, body=%wide.region_2.4_spmd.sunk | while | flops 69203976 | bytes 293085 | solution.py:91
  21.7 1.8 bitcast_reduce_fusion.2
  24.2 1.8 bitcast_reduce_fusion.2
  26.8 1.8 bitcast_reduce_fusion.2
  29.4 1.8 bitcast_reduce_fusion.2
  31.9 1.8 bitcast_reduce_fusion.2
  34.5 1.8 bitcast_reduce_fusion.2
  37.0 1.8 bitcast_reduce_fusion.2
  39.6 1.7 bitcast_reduce_fusion.2
  42.2 1.8 bitcast_reduce_fusion.2
  44.7 1.8 bitcast_reduce_fusion.2
  47.3 1.8 bitcast_reduce_fusion.2
  49.8 1.7 bitcast_reduce_fusion.2
  52.4 1.8 bitcast_reduce_fusion.2
  55.0 1.8 bitcast_reduce_fusion.2
  57.5 1.8 bitcast_reduce_fusion.2
  60.1 1.8 bitcast_reduce_fusion.2
  63.1 21.4 %reduce-scatter.2.cloned.1.call-done = f32[32,512]{1,0:T(8,128)} async-done(((f32[128,512]{1,0:T(8,128)}), f32[32,512]{1,0:T(8,128)}) %reduce-scatter.2.cloned.1.call-update) | async-done | bytes 65552 | tf_op jit(solution)/shard_map/reduce_scatter | solution.py:102
  86.1 3.8 %collective-permute-done = f32[32,512]{1,0:T(8,128)S(1)} collective-permute-done((f32[32,512]{1,0:T(8,128)S(1)}, f32[32,512]{1,0:T(8,128)S(1)}, u32[]{:S(2)}, u32[]{:S(2)}) %collective-permute-start) | collective-permute-done | bytes 65568 | tf_op jit(solution)/shard_map/ppermute | solution.py:115
  90.6 6.0 %collective-permute-done.1 = f32[64,512]{1,0:T(8,128)S(1)} collective-permute-done((f32[64,512]{1,0:T(8,128)S(1)}, f32[64,512]{1,0:T(8,128)S(1)}, u32[]{:S(2)}, u32[]{:S(2)}) %collective-permute-start.1) | collective-permute-done | bytes 131104 | tf_op jit(solution)/shard_map/ppermute | solution.py:115
  96.9 50.3 %while.59 = (s32[]{:T(128)}, f32[512,128]{1,0:T(8,128)S(1)}, f32[64,512]{1,0:T(8,128)S(1)}, bf16[128,8192]{1,0:T(8,128)(2,1)}, bf16[512,128]{1,0:T(8,128)(2,1)S(...) while((s32[]{:T(128)}, f32[512,128]{1,0:T(8,128)S(1)}, ...), condition=%wide.region_9.10_spmd.clone, body=%wide.region_8.9_spmd.clone.sunk | while | flops 135921680 | bytes 3063530 | solution.py:144
  98.5 1.6 fusion.51
  101.7 1.6 fusion.51
  111.1 1.6 fusion.51
  129.9 1.6 fusion.51
  142.5 1.6 fusion.51
  148.0 4.2 %all-gather.1 = f32[2,1,128]{2,1,0:T(1,128)S(1)} all-gather(f32[1,1,128]{2,1,0:T(1,128)S(1)} %get-tuple-element.547), channel_id=1, replica_groups=mesh['grp'=2,'trade'=4,'date'=2,'path'=2] {'date'}, dimensions={0}, use_global_device_ids=true | all-gather | bytes 1536 | tf_op jit(solution)/shard_map/all_gather | solution.py:13
  152.4 3.4 %psum.14 = f32[4,32]{0,1:T(8,128)S(1)} all-reduce(f32[4,32]{0,1:T(8,128)S(1)} %bitcast.153), channel_id=1, replica_groups=mesh['grp'=2,'trade'=4,'date'=2,'path'=2] {'path'}, use_global_device_ids=true, to_apply=%region_7.8 | all-reduce | flops 128 | bytes 1024 | tf_op jit(solution)/shard_map/psum | solution.py:105
  156.4 26.9 %all-reduce.2.cloned.1.call-done = f32[4,128,128]{2,1,0:T(8,128)} async-done(((f32[4,128,128]{2,1,0:T(8,128)}), f32[4,128,128]{2,1,0:T(8,128)}) %all-reduce.2.cloned.1.call-update) | async-done | bytes 262160 | tf_op jit(solution)/shard_map/psum | solution.py:148
  184.3 4.9 %all_gather.19 = f32[2,128,128]{2,1,0:T(8,128)S(1)} all-gather(f32[1,128,128]{2,1,0:T(8,128)S(1)} %add_multiply_fusion), channel_id=1, replica_groups=mesh['grp'=2,'trade'=4,'date'=2,'path'=2] {'date'}, dimensions={0}, use_global_device_ids=true | all-gather | bytes 196608 | tf_op jit(solution)/shard_map/all_gather | solution.py:13
  (162 shorter events, 66.7 us)
Async XLA Ops:
  7.2 13.6 %copy-start = (f32[4,128,128]{2,1,0:T(8,128)S(1)}, f32[4,128,128]{2,1,0:T(8,128)}, u32[]{:S(2)}) copy-start(f32[4,128,128]{2,1,0:T(8,128)} %param.15) | copy-start | bytes 786436
  7.2 77.3 %reduce-scatter.2.cloned.1.call-start = ((), (), s32[]{:S(2)}) async-start(), calls=%async_computation.1 | async-start | bytes 327680 | tf_op jit(solution)/shard_map/reduce_scatter | solution.py:102
  20.8 41.0 %copy-start.2 = (s32[64]{0:T(128)S(1)}, s32[64]{0:T(128)}, u32[]{:S(2)}) copy-start(s32[64]{0:T(128)} %param.19) | copy-start | bytes 772
  20.9 42.2 %copy-start.3 = (f32[4,32]{1,0:T(4,128)S(1)}, f32[4,32]{1,0:T(4,128)}, u32[]{:S(2)}) copy-start(f32[4,32]{1,0:T(4,128)} %param.21) | copy-start | bytes 1540
  20.9 63.7 %copy-start.4 = (f32[32]{0:T(128)S(1)}, f32[32]{0:T(128)}, u32[]{:S(2)}) copy-start(f32[32]{0:T(128)} %param.20) | copy-start | bytes 388
  63.0 120.3 %all-reduce.2.cloned.1.call-start = ((), (), s32[]{:S(2)}) async-start(), calls=%async_computation.2 | async-start | bytes 524288 | tf_op jit(solution)/shard_map/psum | solution.py:148
  85.6 4.3 %collective-permute-start = (f32[32,512]{1,0:T(8,128)S(1)}, f32[32,512]{1,0:T(8,128)S(1)}, u32[]{:S(2)}, u32[]{:S(2)}) collective-permute-start(f32[32,512]{1,0:T(8,128)S(1)} %get-tuple-element.539), channel_id=1, source_target_pairs={{0,12},{4,0},{8,4},{12,8},{1,13},{5,1},{9,5},{13,9},{2,14},{6,2},{... | collective-permute-start | bytes 196616 | tf_op jit(solution)/shard_map/ppermute | solution.py:115
  89.9 6.7 %collective-permute-start.1 = (f32[64,512]{1,0:T(8,128)S(1)}, f32[64,512]{1,0:T(8,128)S(1)}, u32[]{:S(2)}, u32[]{:S(2)}) collective-permute-start(f32[64,512]{1,0:T(8,128)S(1)} %pad_maximum_fusion.2), channel_id=1, source_target_pairs={{0,8},{4,12},{8,0},{12,4},{1,9},{5,13},{9,1},{13,5},{2,10},{6,14},... | collective-permute-start | bytes 393224 | tf_op jit(solution)/shard_map/ppermute | solution.py:115
  147.3 0.7 copy-start.1
Sparse Core Ops, SparseCore 0:
  63.1 21.3 reduce-scatter.1
  148.1 35.1 all-reduce.1
